TPU v7x, 256 devices: a whole 4x4x8 slice. The times are simulated.
256 devices in a mesh: ep: 32 (over z, y), tp: 8 (over x, core).
Axes of the slice: x: 4, y: 4, z: 8, core: 2. Of those that a mesh axis runs over, the one named last changes fastest.
Arguments:
- tokens: bfloat16 [1024, 6144], P('ep', 'tp'), may hold values from -6 to 6
- expert_ids: int32 [1024, 2], P('ep'), may hold values from 0 to 7, all different within a row; in each aligned block of 32 rows (0 to 31, 32 to 63, ...) at most 16 rows name the same one
- combine_weights: float32 [1024, 2], P('ep'), may hold values from 0.1 to 1
- gate_codes: bfloat16 [6144, 65536], P(None, ('ep', 'tp')), may hold values from -6 to 6, as said below
- gate_scales: bfloat16 [192, 65536], P(None, ('ep', 'tp')), as said below
- up_codes: bfloat16 [6144, 65536], P(None, ('ep', 'tp')), may hold values from -6 to 6, as said below
- up_scales: bfloat16 [192, 65536], P(None, ('ep', 'tp')), as said below
- down_codes: bfloat16 [65536, 6144], P(('ep', 'tp')), may hold values from -6 to 6, as said below
- down_scales: bfloat16 [2048, 6144], P(('ep', 'tp')), as said below
Outputs:
- mixed: bfloat16 [1024, 6144], P('ep', 'tp')
Inputs may be any that keep to these rules, and one draw needn't show every extreme that they name: `expert_ids`: each token names 2 different experts. Among the 32 tokens of one index of ep no expert is named more than 16 times, a bound that some block reaches. `gate_codes`: every entry is one of 0, 0.5, 1, 1.5, 2, 3, 4, 6 or its negative. `up_codes`: every entry is one of 0, 0.5, 1, 1.5, 2, 3, 4, 6 or its negative. `down_codes`: every entry is one of 0, 0.5, 1, 1.5, 2, 3, 4, 6 or its negative. `gate_scales`: every entry is a power of two. `up_scales`: every entry is a power of two. `down_scales`: every entry is a power of two.
All inputs are finite; a program needn't handle non-finite values.
Results may differ from a plain program's by a relative error of at most 0.014.
Values may be sent and summed in bfloat16 or wider, within the bound.
A program may use at most 128 MiB of HBM per device.

v0:
```python
import jax
import jax.numpy as jnp
from jax import lax
from jax.sharding import PartitionSpec as P

EXPERTS = 8
CAP = 16


def dequant(code_values, scales):
    count_in, count_out = code_values.shape
    blocks = code_values.reshape(count_in // 32, 32, count_out) * scales[:, None, :]
    return blocks.reshape(count_in, count_out)


def slot_targets(expert_ids):
    count_tokens, count_top = expert_ids.shape
    flat_ids = expert_ids.reshape(-1)
    is_expert = (flat_ids[:, None] == jnp.arange(EXPERTS, dtype=jnp.int32)[None, :]).astype(
        jnp.int32
    )
    before = jnp.cumsum(is_expert, axis=0) - is_expert
    slot_rank = jnp.sum(before * is_expert, axis=1)
    return (flat_ids * CAP + slot_rank).reshape(count_tokens, count_top)


def per_device(
    tokens,
    expert_ids,
    combine_weights,
    gate_codes,
    gate_scales,
    up_codes,
    up_scales,
    down_codes,
    down_scales,
):
    owners = lax.axis_size("ep") // EXPERTS
    gate_matrix = dequant(gate_codes, gate_scales)
    up_matrix = dequant(up_codes, up_scales)
    down_matrix = dequant(down_codes, down_scales)
    target = slot_targets(expert_ids)
    slot_index = jnp.arange(EXPERTS * CAP, dtype=jnp.int32)
    chosen = jnp.zeros((EXPERTS * CAP, target.shape[0]), jnp.float32)
    weighting = jnp.zeros((target.shape[0], EXPERTS * CAP), jnp.float32)
    for column in range(target.shape[1]):
        match_rows = target[:, column][:, None] == slot_index[None, :]
        weighting = weighting + combine_weights[:, column][:, None] * match_rows.astype(jnp.float32)
        chosen = chosen + jnp.transpose(match_rows).astype(jnp.float32)
    chosen = chosen.astype(jnp.bfloat16)
    packed = jnp.dot(chosen, tokens, preferred_element_type=jnp.float32).astype(jnp.bfloat16)
    packed = packed.reshape(EXPERTS, CAP, tokens.shape[1])
    slot_rows = lax.all_gather(
        lax.all_to_all(
            jnp.repeat(packed, owners, axis=0), "ep", split_axis=0, concat_axis=0, tiled=True
        ),
        "tp",
        axis=2,
        tiled=True,
    )
    count_src, count_slots, model_width = slot_rows.shape
    flat_rows = slot_rows.reshape(count_src * count_slots, model_width)
    gate_proj = jnp.dot(flat_rows, gate_matrix, preferred_element_type=jnp.float32)
    up_proj = jnp.dot(flat_rows, up_matrix, preferred_element_type=jnp.float32)
    hidden = (jax.nn.silu(gate_proj) * up_proj).astype(jnp.bfloat16)
    partial_value = jnp.dot(hidden, down_matrix, preferred_element_type=jnp.float32).astype(
        jnp.bfloat16
    )
    partial_value = partial_value.reshape(count_src, count_slots, model_width)
    reduced = lax.psum_scatter(
        partial_value.astype(jnp.float32).astype(jnp.bfloat16),
        "tp",
        scatter_dimension=2,
        tiled=True,
    ).astype(jnp.float32)
    returned = lax.all_to_all(
        reduced.astype(jnp.bfloat16), "ep", split_axis=0, concat_axis=0, tiled=True
    ).astype(reduced.dtype)
    feature_width = returned.shape[2]
    grouped = returned.reshape(EXPERTS, owners, CAP, feature_width)
    per_expert = jnp.sum(grouped, axis=1).reshape(EXPERTS * CAP, feature_width)
    mixed_out = jnp.dot(weighting, per_expert, preferred_element_type=jnp.float32)
    return mixed_out.astype(jnp.bfloat16)


def solution(mesh):
    placed = (
        P("ep", "tp"),
        P("ep", None),
        P("ep", None),
        P(None, ("ep", "tp")),
        P(None, ("ep", "tp")),
        P(None, ("ep", "tp")),
        P(None, ("ep", "tp")),
        P(("ep", "tp"), None),
        P(("ep", "tp"), None),
    )
    return jax.shard_map(
        per_device, mesh=mesh, in_specs=placed, out_specs=P("ep", "tp"), check_vma=False
    )
```

profile of v0, /device:TPU:8, one launch (start us, length us, event | category | flops | bytes accessed | tf_op | source)
XLA Modules:
  0.0 188.0 jit_solution(12755171529070535130)
XLA Ops:
  6.5 0.9 copy.16
  7.5 0.1 eq.59
  7.6 0.1 fusion.9
  7.6 0.1 reduce_window_sum.11
  7.7 0.2 select_reduce_fusion
  7.9 0.1 reduce_sum.21
  8.0 0.1 copy.17
  8.1 0.7 multiply_add_fusion
  8.8 0.2 convolution_convert_fusion.1
  9.0 0.1 broadcast_in_dim.2
  9.1 34.1 %all_to_all.10 = bf16[32,16,768]{2,1,0:T(8,128)(2,1)} all-to-all(bf16[32,16,768]{2,1,0:T(8,128)(2,1)S(1)} %bitcast.30), channel_id=1, replica_groups=mesh['ep'=32,'tp'=8] {'ep'}, dimensions={0} | all-to-all | bytes 1572864 | tf_op jit(solution)/shard_map/all_to_all | solution.py:54
  43.2 1.9 %bitcast_multiply_fusion.2 = bf16[6144,256]{1,0:T(8,128)(2,1)} fusion(bf16[6144,256]{1,0:T(8,128)(2,1)S(1)} %copy-done.1, bf16[192,256]{1,0:T(8,128)(2,1)S(1)} %copy-done.4), kind=kLoop, calls=%fused_computation.3 | loop fusion | flops 1572864 | bytes 6389760 | tf_op jit(solution)/shard_map/mul | solution.py:12
  45.2 1.1 copy-done.2
  46.3 0.3 bitcast_multiply_fusion
  46.6 1.6 copy-done.3
  48.2 1.9 %bitcast_multiply_fusion.1 = bf16[6144,256]{1,0:T(8,128)(2,1)} fusion(bf16[6144,256]{1,0:T(8,128)(2,1)S(1)} %copy-done.3, bf16[192,256]{1,0:T(8,128)(2,1)S(1)} %copy-done.6), kind=kLoop, calls=%fused_computation.2 | loop fusion | flops 1572864 | bytes 6389760 | tf_op jit(solution)/shard_map/mul | solution.py:12
  50.1 33.4 %all-gather.2.cloned.1.call-done = bf16[32,16,6144]{2,1,0:T(8,128)(2,1)} async-done(((bf16[32,16,768]{2,1,0:T(8,128)(2,1)}), bf16[32,16,6144]{2,1,0:T(8,128)(2,1)}) %all-gather.2.cloned.1.call-update) | async-done | bytes 6291472 | tf_op jit(solution)/shard_map/all_gather | solution.py:53
  83.4 6.3 %fusion.20 = f32[512,256]{1,0:T(8,128)} fusion(bf16[512,6144]{1,0:T(8,128)(2,1)} %bitcast.33, bf16[6144,256]{1,0:T(8,128)(2,1)} %bitcast_multiply_fusion.2), kind=kOutput, calls=%fused_computation.40 | convolution fusion | flops 1610612736 | bytes 9961472 | tf_op jit(solution)/shard_map/dot_general | solution.py:63
  89.7 13.1 %convolution_convert_fusion = bf16[512,6144]{1,0:T(8,128)(2,1)} fusion(bf16[256,6144]{1,0:T(8,128)(2,1)S(1)} %bitcast_multiply_fusion, bf16[512,6144]{1,0:T(8,128)(2,1)} %bitcast.34, bf16[6144,256]{1,0:T(8,128)(2,1)} %bitcast_multiply_fusion.1, f32[512,256]{1,0:T(8,128)} %fusion.20), kind=kOutput, calls=%fused_computation | convolution fusion | flops 3225157632 | bytes 19398656 | tf_op jit(solution)/shard_map/dot_general | solution.py:66
  102.8 45.3 %reduce-scatter.2.cloned.1.call-done = bf16[32,16,768]{2,1,0:T(8,128)(2,1)} async-done(((bf16[32,16,6144]{2,1,0:T(8,128)(2,1)}), bf16[32,16,768]{2,1,0:T(8,128)(2,1)}) %reduce-scatter.2.cloned.1.call-update) | async-done | bytes 786448 | tf_op jit(solution)/shard_map/reduce_scatter | solution.py:70
  148.1 10.2 %all-to-all-start.1 = ((bf16[32,16,768]{2,1,0:T(8,128)(2,1)}), bf16[32,16,768]{2,1,0:T(8,128)(2,1)S(1)}, u32[]{:S(2)}, u32[]{:S(2)}) async-start(bf16[32,16,768]{2,1,0:T(8,128)(2,1)} %reduce-scatter.2.cloned.1.call-done), calls=%async_computation.2 | async-start | bytes 1572864 | tf_op jit(solution)/shard_map/all_to_all | solution.py:76
  158.3 21.9 %all-to-all-done.1 = bf16[32,16,768]{2,1,0:T(8,128)(2,1)S(1)} async-done(((bf16[32,16,768]{2,1,0:T(8,128)(2,1)}), bf16[32,16,768]{2,1,0:T(8,128)(2,1)S(1)}, u32[]{:S(2)}, u32[]{:S(2)}) %all-to-all-start.1) | async-done | bytes 786464 | tf_op jit(solution)/shard_map/all_to_all | solution.py:76
  180.2 0.1 convert_reduce_fusion
  180.3 0.8 convolution_convert_fusion.2
  (20 shorter events, 0.1 us)
Async XLA Ops:
  6.5 2.3 %copy-start = (bf16[32,768]{1,0:T(8,128)(2,1)S(1)}, bf16[32,768]{1,0:T(8,128)(2,1)}, u32[]{:S(2)}) copy-start(bf16[32,768]{1,0:T(8,128)(2,1)} %param.9) | copy-start | bytes 147460
  6.5 36.7 %copy-start.1 = (bf16[6144,256]{1,0:T(8,128)(2,1)S(1)}, bf16[6144,256]{1,0:T(8,128)(2,1)}, u32[]{:S(2)}) copy-start(bf16[6144,256]{1,0:T(8,128)(2,1)} %param.12) | copy-start | bytes 9437188
  6.5 36.7 %copy-start.4 = (bf16[192,256]{1,0:T(8,128)(2,1)S(1)}, bf16[192,256]{1,0:T(8,128)(2,1)}, u32[]{:S(2)}) copy-start(bf16[192,256]{1,0:T(8,128)(2,1)} %param.13) | copy-start | bytes 294916
  6.5 76.9 %all-gather.2.cloned.1.call-start = ((), (), s32[]{:S(2)}) async-start(), calls=%async_computation.3 | async-start | bytes 7077888 | tf_op jit(solution)/shard_map/all_gather | solution.py:53
  43.2 2.0 %copy-start.5 = (bf16[8,6144]{1,0:T(8,128)(2,1)S(1)}, bf16[8,6144]{1,0:T(8,128)(2,1)}, u32[]{:S(2)}) copy-start(bf16[8,6144]{1,0:T(8,128)(2,1)} %param.17) | copy-start | bytes 294916
  43.2 104.9 %reduce-scatter.2.cloned.1.call-start = ((), (), s32[]{:S(2)}) async-start(), calls=%async_computation.4 | async-start | bytes 7077888 | tf_op jit(solution)/shard_map/reduce_scatter | solution.py:70
  43.2 3.0 %copy-start.2 = (bf16[256,6144]{1,0:T(8,128)(2,1)S(1)}, bf16[256,6144]{1,0:T(8,128)(2,1)}, u32[]{:S(2)}) copy-start(bf16[256,6144]{1,0:T(8,128)(2,1)} %param.16) | copy-start | bytes 9437188
  46.3 1.9 %copy-start.3 = (bf16[6144,256]{1,0:T(8,128)(2,1)S(1)}, bf16[6144,256]{1,0:T(8,128)(2,1)}, u32[]{:S(2)}) copy-start(bf16[6144,256]{1,0:T(8,128)(2,1)} %param.14) | copy-start | bytes 9437188
  46.3 1.9 %copy-start.6 = (bf16[192,256]{1,0:T(8,128)(2,1)S(1)}, bf16[192,256]{1,0:T(8,128)(2,1)}, u32[]{:S(2)}) copy-start(bf16[192,256]{1,0:T(8,128)(2,1)} %param.15) | copy-start | bytes 294916
  102.8 55.5 %copy-start.7 = (f32[32,2]{0,1:T(2,128)S(1)}, f32[32,2]{0,1:T(2,128)}, u32[]{:S(2)}) copy-start(f32[32,2]{0,1:T(2,128)} %param.11) | copy-start | bytes 772
  148.1 32.1 %all-to-all-start.1 = ((bf16[32,16,768]{2,1,0:T(8,128)(2,1)}), bf16[32,16,768]{2,1,0:T(8,128)(2,1)S(1)}, u32[]{:S(2)}, u32[]{:S(2)}) async-start(bf16[32,16,768]{2,1,0:T(8,128)(2,1)} %reduce-scatter.2.cloned.1.call-done), calls=%async_computation.2 | async-start | bytes 1572864 | tf_op jit(solution)/shard_map/all_to_all | solution.py:76
Sparse Core Ops, SparseCore 0:
  43.3 40.1 all-gather.1
  102.9 45.1 reduce-scatter.1
where the time goes:
time: 188 us
  waiting for transfers between devices  101 us (54%)
  blocking collectives  34.1 us (18%)
  matrix products  20.4 us (11%)
  between operations  13.5 us (7%)
  starting transfers between devices  10.2 us (5%)
  other arithmetic  5.26 us (3%)
  local copies, waits for them, and re-layouts  3.99 us (2%)
    reduce_scatter x1, waiting for transfers between devices, per_device(): lax.psum_scatter(partial_value.astype(jnp.float32).astype(jnp.bfloat16),...  45.3 us
    all_to_all x1, blocking collectives, per_device(): lax.all_to_all(jnp.repeat(packed, owners, axis=0), 'ep', split_axis=0, co...  34.1 us
    all_gather x1, waiting for transfers between devices, per_device(): lax.all_gather(lax.all_to_all(jnp.repeat(packed, owners, axis=0), 'ep', s...  33.4 us
    all_to_all x1, waiting for transfers between devices, per_device(): lax.all_to_all(reduced.astype(jnp.bfloat16), 'ep', split_axis=0, concat_a...  21.9 us
    dot_general x1, matrix products, per_device(): jnp.dot(hidden, down_matrix, preferred_element_type=jnp.float32)  13.1 us
    all_to_all x1, starting transfers between devices, per_device(): lax.all_to_all(reduced.astype(jnp.bfloat16), 'ep', split_axis=0, concat_a...  10.2 us
    dot_general x1, matrix products, per_device(): jnp.dot(flat_rows, gate_matrix, preferred_element_type=jnp.float32)  6.3 us
    mul x3, other arithmetic, dequant(): code_values.reshape(count_in // 32, 32, count_out) * scales[:, None, :]  4.1 us
  transfers between devices with their start and end apart: 3, of which 3 were waited for; matrix products, arithmetic and copies ran while one was open for 2% of the time, Pallas kernels for 0%

commit v1 on v0

--- a/solution.py
+++ b/solution.py
@@ -50,14 +50,17 @@
     chosen = chosen.astype(jnp.bfloat16)
     packed = jnp.dot(chosen, tokens, preferred_element_type=jnp.float32).astype(jnp.bfloat16)
     packed = packed.reshape(EXPERTS, CAP, tokens.shape[1])
-    slot_rows = lax.all_gather(
-        lax.all_to_all(
-            jnp.repeat(packed, owners, axis=0), "ep", split_axis=0, concat_axis=0, tiled=True
-        ),
-        "tp",
-        axis=2,
-        tiled=True,
+    value = lax.all_to_all(
+        jnp.repeat(packed, owners, axis=0), "ep", split_axis=0, concat_axis=0, tiled=True
     )
+    ways = lax.axis_size("tp")
+    pieces = [value]
+    for far in range(1, ways):
+        pieces.append(
+            lax.ppermute(pieces[far - 1], "tp", [(d, (d - 1) % ways) for d in range(ways)])
+        )
+    line = jnp.concatenate(pieces, axis=2)
+    slot_rows = jnp.roll(line, lax.axis_index("tp") * value.shape[2], axis=2)
     count_src, count_slots, model_width = slot_rows.shape
     flat_rows = slot_rows.reshape(count_src * count_slots, model_width)
     gate_proj = jnp.dot(flat_rows, gate_matrix, preferred_element_type=jnp.float32)

time: 188 us -> 250 us (1.33)
  local copies, waits for them, and re-layouts: 3.99 us -> 32.4 us
  starting transfers between devices: 10.2 us -> 29.6 us
  waiting for transfers between devices: 101 us -> 114 us
  other arithmetic: 5.26 us -> 9.11 us
  matrix products: 20.4 us -> 16.7 us
    ppermute x0 -> x7, waiting for transfers between devices: none -> 49.9 us  [per_device(): lax.ppermute(pieces[far - 1], 'tp', [(d, (d - 1) % ways) for d in range(w...]
    all_gather x1 -> x0, waiting for transfers between devices: 33.4 us -> none  [per_device(): lax.all_gather(lax.all_to_all(jnp.repeat(packed, owners, axis=0), 'ep', s...]
    unnamed x17 -> x32, local copies, waits for them, and re-layouts: 3.64 us -> 24 us
    ppermute x0 -> x7, starting transfers between devices: none -> 19.4 us  [per_device(): lax.ppermute(pieces[far - 1], 'tp', [(d, (d - 1) % ways) for d in range(w...]
    dynamic_slice x0 -> x1, local copies, waits for them, and re-layouts: none -> 7.02 us  [per_device(): slot_rows = jnp.roll(line, lax.axis_index('tp') * value.shape[2], axis=2)]
    mul x3, other arithmetic: 4.1 us -> 7.96 us  [dequant(): code_values.reshape(count_in // 32, 32, count_out) * scales[:, None, :]]
    dot_general x1, matrix products: 6.3 us -> 2.59 us  [per_device(): jnp.dot(flat_rows, gate_matrix, preferred_element_type=jnp.float32)]
    reduce_scatter x1, waiting for transfers between devices: 45.3 us -> 42.4 us  [per_device(): lax.psum_scatter(partial_value.astype(jnp.float32).astype(jnp.bfloat16),...]
  transfers between devices with their start and end apart: 3 -> 9, of which waited for: 3 -> 9; matrix products, arithmetic and copies ran while one was open for 2% -> 7% of each run, Pallas kernels for 0% -> 0%
where the time goes in v1:
time: 250 us; the launch traced here: 249 us
  waiting for transfers between devices  114 us (46%)
  blocking collectives  33.9 us (14%)
  local copies, waits for them, and re-layouts  32.4 us (13%)
  starting transfers between devices  29.6 us (12%)
  matrix products  16.7 us (7%)
  between operations  13.5 us (5%)
  other arithmetic  9.11 us (4%)
    ppermute x7, waiting for transfers between devices, per_device(): lax.ppermute(pieces[far - 1], 'tp', [(d, (d - 1) % ways) for d in range(w...  49.9 us
    reduce_scatter x1, waiting for transfers between devices, per_device(): lax.psum_scatter(partial_value.astype(jnp.float32).astype(jnp.bfloat16),...  42.4 us
    all_to_all x1, blocking collectives, per_device(): lax.all_to_all(jnp.repeat(packed, owners, axis=0), 'ep', split_axis=0, co...  33.9 us
    unnamed x32, local copies, waits for them, and re-layouts  24 us
    all_to_all x1, waiting for transfers between devices, per_device(): lax.all_to_all(reduced.astype(jnp.bfloat16), 'ep', split_axis=0, concat_a...  21.9 us
    ppermute x7, starting transfers between devices, per_device(): lax.ppermute(pieces[far - 1], 'tp', [(d, (d - 1) % ways) for d in range(w...  19.4 us
    dot_general x1, matrix products, per_device(): jnp.dot(hidden, down_matrix, preferred_element_type=jnp.float32)  13.1 us
    all_to_all x1, starting transfers between devices, per_device(): lax.all_to_all(reduced.astype(jnp.bfloat16), 'ep', split_axis=0, concat_a...  10.2 us
  transfers between devices with their start and end apart: 9, of which 9 were waited for; matrix products, arithmetic and copies ran while one was open for 7% of the time, Pallas kernels for 0%

profile of v1, /device:TPU:8, one launch (start us, length us, event | category | flops | bytes accessed | tf_op | source)
XLA Modules:
  0.0 249.5 jit_solution(1958004501023300570)
XLA Ops:
  8.9 33.9 %all_to_all.10 = bf16[32,16,768]{2,1,0:T(8,128)(2,1)S(1)} all-to-all(bf16[32,16,768]{2,1,0:T(8,128)(2,1)S(1)} %bitcast.32), channel_id=1, replica_groups=mesh['ep'=32,'tp'=8] {'ep'}, dimensions={0} | all-to-all | bytes 1572864 | tf_op jit(solution)/shard_map/all_to_all | solution.py:53
  43.5 9.5 %collective-permute-done = bf16[32,16,768]{2,1,0:T(8,128)(2,1)S(1)} collective-permute-done((bf16[32,16,768]{2,1,0:T(8,128)(2,1)S(1)}, bf16[32,16,768]{2,1,0:T(8,128)(2,1)S(1)}, u32[]{:S(2)}, u32[]{:S(2)}) %collective-permute-start) | collective-permute-done | bytes 786464 | tf_op jit(solution)/shard_map/ppermute | solution.py:60
  53.0 3.1 %collective-permute-start.1 = (bf16[32,16,768]{2,1,0:T(8,128)(2,1)S(1)}, bf16[32,16,768]{2,1,0:T(8,128)(2,1)S(1)}, u32[]{:S(2)}, u32[]{:S(2)}) collective-permute-start(bf16[32,16,768]{2,1,0:T(8,128)(2,1)S(1)} %collective-permute-done), channel_id=1, source_target_pairs={{0,7},{1,0},{2,1},{3,2},{4,3},{5,4},{6,5},{7,6},{8,15},{9,8},{10,9... | collective-permute-start | bytes 2359304 | tf_op jit(solution)/shard_map/ppermute | solution.py:60
  56.1 9.5 %collective-permute-done.1 = bf16[32,16,768]{2,1,0:T(8,128)(2,1)S(1)} collective-permute-done((bf16[32,16,768]{2,1,0:T(8,128)(2,1)S(1)}, bf16[32,16,768]{2,1,0:T(8,128)(2,1)S(1)}, u32[]{:S(2)}, u32[]{:S(2)}) %collective-permute-start.1) | collective-permute-done | bytes 786464 | tf_op jit(solution)/shard_map/ppermute | solution.py:60
  65.6 3.1 %collective-permute-start.2 = (bf16[32,16,768]{2,1,0:T(8,128)(2,1)S(1)}, bf16[32,16,768]{2,1,0:T(8,128)(2,1)S(1)}, u32[]{:S(2)}, u32[]{:S(2)}) collective-permute-start(bf16[32,16,768]{2,1,0:T(8,128)(2,1)S(1)} %collective-permute-done.1), channel_id=1, source_target_pairs={{0,7},{1,0},{2,1},{3,2},{4,3},{5,4},{6,5},{7,6},{8,15},{9,8},{10,9... | collective-permute-start | bytes 2359304 | tf_op jit(solution)/shard_map/ppermute | solution.py:60
  68.7 9.5 %collective-permute-done.2 = bf16[32,16,768]{2,1,0:T(8,128)(2,1)S(1)} collective-permute-done((bf16[32,16,768]{2,1,0:T(8,128)(2,1)S(1)}, bf16[32,16,768]{2,1,0:T(8,128)(2,1)S(1)}, u32[]{:S(2)}, u32[]{:S(2)}) %collective-permute-start.2) | collective-permute-done | bytes 786464 | tf_op jit(solution)/shard_map/ppermute | solution.py:60
  78.2 3.1 %collective-permute-start.3 = (bf16[32,16,768]{2,1,0:T(8,128)(2,1)S(1)}, bf16[32,16,768]{2,1,0:T(8,128)(2,1)S(1)}, u32[]{:S(2)}, u32[]{:S(2)}) collective-permute-start(bf16[32,16,768]{2,1,0:T(8,128)(2,1)S(1)} %collective-permute-done.2), channel_id=1, source_target_pairs={{0,7},{1,0},{2,1},{3,2},{4,3},{5,4},{6,5},{7,6},{8,15},{9,8},{10,9... | collective-permute-start | bytes 2359304 | tf_op jit(solution)/shard_map/ppermute | solution.py:60
  81.4 9.5 %collective-permute-done.3 = bf16[32,16,768]{2,1,0:T(8,128)(2,1)S(1)} collective-permute-done((bf16[32,16,768]{2,1,0:T(8,128)(2,1)S(1)}, bf16[32,16,768]{2,1,0:T(8,128)(2,1)S(1)}, u32[]{:S(2)}, u32[]{:S(2)}) %collective-permute-start.3) | collective-permute-done | bytes 786464 | tf_op jit(solution)/shard_map/ppermute | solution.py:60
  91.7 3.1 %collective-permute-start.4 = (bf16[32,16,768]{2,1,0:T(8,128)(2,1)S(1)}, bf16[32,16,768]{2,1,0:T(8,128)(2,1)}, u32[]{:S(2)}, u32[]{:S(2)}) collective-permute-start(bf16[32,16,768]{2,1,0:T(8,128)(2,1)S(1)} %collective-permute-done.3), channel_id=1, source_target_pairs={{0,7},{1,0},{2,1},{3,2},{4,3},{5,4},{6,5},{7,6},{8,15},{9,8},{10,9... | collective-permute-start | bytes 2359304 | tf_op jit(solution)/shard_map/ppermute | solution.py:60
  94.9 9.5 %collective-permute-done.4 = bf16[32,16,768]{2,1,0:T(8,128)(2,1)} collective-permute-done((bf16[32,16,768]{2,1,0:T(8,128)(2,1)S(1)}, bf16[32,16,768]{2,1,0:T(8,128)(2,1)}, u32[]{:S(2)}, u32[]{:S(2)}) %collective-permute-start.4) | collective-permute-done | bytes 786464 | tf_op jit(solution)/shard_map/ppermute | solution.py:60
  104.4 3.2 %collective-permute-start.5 = (bf16[32,16,768]{2,1,0:T(8,128)(2,1)}, bf16[32,16,768]{2,1,0:T(8,128)(2,1)}, u32[]{:S(2)}, u32[]{:S(2)}) collective-permute-start(bf16[32,16,768]{2,1,0:T(8,128)(2,1)} %collective-permute-done.4), channel_id=1, source_target_pairs={{0,7},{1,0},{2,1},{3,2},{4,3},{5,4},{6,5},{7,6},{8,15},{9,8},{10,9... | collective-permute-start | bytes 2359304 | tf_op jit(solution)/shard_map/ppermute | solution.py:60
  107.6 2.3 bitcast_multiply_fusion.2
  109.9 3.8 %bitcast_multiply_fusion = bf16[256,6144]{1,0:T(8,128)(2,1)} fusion(bf16[256,6144]{1,0:T(8,128)(2,1)} %param.16, bf16[8,6144]{1,0:T(8,128)(2,1)} %param.17), kind=kLoop, calls=%fused_computation.1 | loop fusion | flops 1572864 | bytes 6389760 | tf_op jit(solution)/shard_map/mul | solution.py:12
  117.4 3.1 %collective-permute-start.6 = (bf16[32,16,768]{2,1,0:T(8,128)(2,1)}, bf16[32,16,768]{2,1,0:T(8,128)(2,1)S(1)}, u32[]{:S(2)}, u32[]{:S(2)}) collective-permute-start(bf16[32,16,768]{2,1,0:T(8,128)(2,1)} %collective-permute-done.5), channel_id=1, source_target_pairs={{0,7},{1,0},{2,1},{3,2},{4,3},{5,4},{6,5},{7,6},{8,15},{9,8},{10,9... | collective-permute-start | bytes 2359304 | tf_op jit(solution)/shard_map/ppermute | solution.py:60
  124.5 2.1 constant_dynamic-update-slice_fusion.10
  126.6 2.2 constant_dynamic-update-slice_fusion.9
  138.5 2.3 constant_dynamic-update-slice_fusion.1
  141.7 7.0 %constant_dynamic-slice_fusion = bf16[32,16,6144]{2,1,0:T(8,128)(2,1)S(1)} fusion(bf16[32,16,12288]{2,1,0:T(8,128)(2,1)} %constant_dynamic-update-slice_fusion, s32[]{:T(128)S(6)} %select_n.14), kind=kLoop, calls=%fused_computation.48 | loop fusion | bytes 12582916 | tf_op jit(solution)/shard_map/jit(_roll_dynamic)/dynamic_slice | solution.py:63
  148.8 2.7 %copy-done.1 = bf16[32,16,6144]{2,1,0:T(8,128)(2,1)} copy-done((bf16[32,16,6144]{2,1,0:T(8,128)(2,1)}, bf16[32,16,6144]{2,1,0:T(8,128)(2,1)S(1)}, u32[]{:S(2)}) %copy-start.1) | copy-done | bytes 6291480
  151.4 2.6 %fusion.16 = f32[512,256]{1,0:T(8,128)} fusion(bf16[512,6144]{1,0:T(8,128)(2,1)S(1)} %bitcast.30, bf16[6144,256]{1,0:T(8,128)(2,1)S(1)} %bitcast_multiply_fusion.2), kind=kOutput, calls=%fused_computation.52 | convolution fusion | flops 1610612736 | bytes 9961472 | tf_op jit(solution)/shard_map/dot_general | solution.py:66
  154.0 13.1 %convolution_convert_fusion = bf16[512,6144]{1,0:T(8,128)(2,1)} fusion(bf16[256,6144]{1,0:T(8,128)(2,1)S(1)} %copy-done.3, f32[512,256]{1,0:T(8,128)} %fusion.16, bf16[512,6144]{1,0:T(8,128)(2,1)} %bitcast.31, bf16[6144,256]{1,0:T(8,128)(2,1)} %bitcast_multiply_fusion.1), kind=kOutput, calls=%fused_computation | convolution fusion | flops 3225157632 | bytes 19398656 | tf_op jit(solution)/shard_map/dot_general | solution.py:69
  167.1 42.4 %reduce-scatter.2.cloned.1.call-done = bf16[32,16,768]{2,1,0:T(8,128)(2,1)} async-done(((bf16[32,16,6144]{2,1,0:T(8,128)(2,1)}), bf16[32,16,768]{2,1,0:T(8,128)(2,1)}) %reduce-scatter.2.cloned.1.call-update) | async-done | bytes 786448 | tf_op jit(solution)/shard_map/reduce_scatter | solution.py:73
  209.6 10.2 %all-to-all-start.1 = ((bf16[32,16,768]{2,1,0:T(8,128)(2,1)}), bf16[32,16,768]{2,1,0:T(8,128)(2,1)S(1)}, u32[]{:S(2)}, u32[]{:S(2)}) async-start(bf16[32,16,768]{2,1,0:T(8,128)(2,1)} %reduce-scatter.2.cloned.1.call-done), calls=%async_computation.2 | async-start | bytes 1572864 | tf_op jit(solution)/shard_map/all_to_all | solution.py:79
  219.8 21.9 %all-to-all-done.1 = bf16[32,16,768]{2,1,0:T(8,128)(2,1)S(1)} async-done(((bf16[32,16,768]{2,1,0:T(8,128)(2,1)}), bf16[32,16,768]{2,1,0:T(8,128)(2,1)S(1)}, u32[]{:S(2)}, u32[]{:S(2)}) %all-to-all-start.1) | async-done | bytes 786464 | tf_op jit(solution)/shard_map/all_to_all | solution.py:79
  (48 shorter events, 23.2 us)
Async XLA Ops:
  6.5 2.2 copy-start
  6.5 107.1 %copy-start.6 = (bf16[192,256]{1,0:T(8,128)(2,1)S(1)}, bf16[192,256]{1,0:T(8,128)(2,1)}, u32[]{:S(2)}) copy-start(bf16[192,256]{1,0:T(8,128)(2,1)} %param.15) | copy-start | bytes 294916
  6.5 203.0 %reduce-scatter.2.cloned.1.call-start = ((), (), s32[]{:S(2)}) async-start(), calls=%async_computation.3 | async-start | bytes 7077888 | tf_op jit(solution)/shard_map/reduce_scatter | solution.py:73
  42.9 10.1 %collective-permute-start = (bf16[32,16,768]{2,1,0:T(8,128)(2,1)S(1)}, bf16[32,16,768]{2,1,0:T(8,128)(2,1)S(1)}, u32[]{:S(2)}, u32[]{:S(2)}) collective-permute-start(bf16[32,16,768]{2,1,0:T(8,128)(2,1)S(1)} %all_to_all.10), channel_id=1, source_target_pairs={{0,7},{1,0},{2,1},{3,2},{4,3},{5,4},{6,5},{7,6},{8,15},{9,8},{10,9... | collective-permute-start | bytes 2359304 | tf_op jit(solution)/shard_map/ppermute | solution.py:60
  53.0 12.6 %collective-permute-start.1 = (bf16[32,16,768]{2,1,0:T(8,128)(2,1)S(1)}, bf16[32,16,768]{2,1,0:T(8,128)(2,1)S(1)}, u32[]{:S(2)}, u32[]{:S(2)}) collective-permute-start(bf16[32,16,768]{2,1,0:T(8,128)(2,1)S(1)} %collective-permute-done), channel_id=1, source_target_pairs={{0,7},{1,0},{2,1},{3,2},{4,3},{5,4},{6,5},{7,6},{8,15},{9,8},{10,9... | collective-permute-start | bytes 2359304 | tf_op jit(solution)/shard_map/ppermute | solution.py:60
  65.6 12.6 %collective-permute-start.2 = (bf16[32,16,768]{2,1,0:T(8,128)(2,1)S(1)}, bf16[32,16,768]{2,1,0:T(8,128)(2,1)S(1)}, u32[]{:S(2)}, u32[]{:S(2)}) collective-permute-start(bf16[32,16,768]{2,1,0:T(8,128)(2,1)S(1)} %collective-permute-done.1), channel_id=1, source_target_pairs={{0,7},{1,0},{2,1},{3,2},{4,3},{5,4},{6,5},{7,6},{8,15},{9,8},{10,9... | collective-permute-start | bytes 2359304 | tf_op jit(solution)/shard_map/ppermute | solution.py:60
  78.2 12.6 %collective-permute-start.3 = (bf16[32,16,768]{2,1,0:T(8,128)(2,1)S(1)}, bf16[32,16,768]{2,1,0:T(8,128)(2,1)S(1)}, u32[]{:S(2)}, u32[]{:S(2)}) collective-permute-start(bf16[32,16,768]{2,1,0:T(8,128)(2,1)S(1)} %collective-permute-done.2), channel_id=1, source_target_pairs={{0,7},{1,0},{2,1},{3,2},{4,3},{5,4},{6,5},{7,6},{8,15},{9,8},{10,9... | collective-permute-start | bytes 2359304 | tf_op jit(solution)/shard_map/ppermute | solution.py:60
  90.9 0.9 copy-start.4
  91.7 12.6 %collective-permute-start.4 = (bf16[32,16,768]{2,1,0:T(8,128)(2,1)S(1)}, bf16[32,16,768]{2,1,0:T(8,128)(2,1)}, u32[]{:S(2)}, u32[]{:S(2)}) collective-permute-start(bf16[32,16,768]{2,1,0:T(8,128)(2,1)S(1)} %collective-permute-done.3), channel_id=1, source_target_pairs={{0,7},{1,0},{2,1},{3,2},{4,3},{5,4},{6,5},{7,6},{8,15},{9,8},{10,9... | collective-permute-start | bytes 2359304 | tf_op jit(solution)/shard_map/ppermute | solution.py:60
  104.4 13.0 %collective-permute-start.5 = (bf16[32,16,768]{2,1,0:T(8,128)(2,1)}, bf16[32,16,768]{2,1,0:T(8,128)(2,1)}, u32[]{:S(2)}, u32[]{:S(2)}) collective-permute-start(bf16[32,16,768]{2,1,0:T(8,128)(2,1)} %collective-permute-done.4), channel_id=1, source_target_pairs={{0,7},{1,0},{2,1},{3,2},{4,3},{5,4},{6,5},{7,6},{8,15},{9,8},{10,9... | collective-permute-start | bytes 2359304 | tf_op jit(solution)/shard_map/ppermute | solution.py:60
  107.6 6.1 %copy-start.2 = (bf16[6144,256]{1,0:T(8,128)(2,1)S(1)}, bf16[6144,256]{1,0:T(8,128)(2,1)}, u32[]{:S(2)}) copy-start(bf16[6144,256]{1,0:T(8,128)(2,1)} %param.14) | copy-start | bytes 9437188
  107.6 15.9 %copy-start.5 = (bf16[32,16,768]{2,1,0:T(8,128)(2,1)S(1)}, bf16[32,16,768]{2,1,0:T(8,128)(2,1)}, u32[]{:S(2)}) copy-start(bf16[32,16,768]{2,1,0:T(8,128)(2,1)} %copy-done.4) | copy-start | bytes 2359300
  117.4 12.9 %collective-permute-start.6 = (bf16[32,16,768]{2,1,0:T(8,128)(2,1)}, bf16[32,16,768]{2,1,0:T(8,128)(2,1)S(1)}, u32[]{:S(2)}, u32[]{:S(2)}) collective-permute-start(bf16[32,16,768]{2,1,0:T(8,128)(2,1)} %collective-permute-done.5), channel_id=1, source_target_pairs={{0,7},{1,0},{2,1},{3,2},{4,3},{5,4},{6,5},{7,6},{8,15},{9,8},{10,9... | collective-permute-start | bytes 2359304 | tf_op jit(solution)/shard_map/ppermute | solution.py:60
  141.7 12.3 %copy-start.3 = (bf16[256,6144]{1,0:T(8,128)(2,1)S(1)}, bf16[256,6144]{1,0:T(8,128)(2,1)}, u32[]{:S(2)}) copy-start(bf16[256,6144]{1,0:T(8,128)(2,1)} %bitcast_multiply_fusion) | copy-start | bytes 9437188
  148.8 2.7 %copy-start.1 = (bf16[32,16,6144]{2,1,0:T(8,128)(2,1)}, bf16[32,16,6144]{2,1,0:T(8,128)(2,1)S(1)}, u32[]{:S(2)}) copy-start(bf16[32,16,6144]{2,1,0:T(8,128)(2,1)S(1)} %constant_dynamic-slice_fusion) | copy-start | bytes 18874372
  154.0 65.7 %copy-start.7 = (f32[32,2]{0,1:T(2,128)S(1)}, f32[32,2]{0,1:T(2,128)}, u32[]{:S(2)}) copy-start(f32[32,2]{0,1:T(2,128)} %param.11) | copy-start | bytes 772
  209.6 32.1 %all-to-all-start.1 = ((bf16[32,16,768]{2,1,0:T(8,128)(2,1)}), bf16[32,16,768]{2,1,0:T(8,128)(2,1)S(1)}, u32[]{:S(2)}, u32[]{:S(2)}) async-start(bf16[32,16,768]{2,1,0:T(8,128)(2,1)} %reduce-scatter.2.cloned.1.call-done), calls=%async_computation.2 | async-start | bytes 1572864 | tf_op jit(solution)/shard_map/all_to_all | solution.py:79
Sparse Core Ops, SparseCore 0:
  167.3 42.2 reduce-scatter.1
